TPU v7x, 32 devices: a whole 2x2x4 slice. The times are simulated.
32 devices in a mesh: grp: 2 (over y), seq: 4 (over z), tp: 2 (over x), pr: 2 (over core).
Axes of the slice: x: 2, y: 2, z: 4, core: 2. Of those that a mesh axis runs over, the one named last changes fastest.
Arguments:
- dna_feats: bfloat16 [2048, 768], P(('grp', 'seq', 'pr'), 'tp'), parts along dimension 0, may hold values from -6 to 6
- conv_w: bfloat16 [5, 768, 1536], P(None, 'pr', 'tp'), may hold values from -0.09375 to 0.09375
- conv_gain: float32 [1536], P('tp'), may hold values from 0.1 to 1.9
- attn_gain: float32 [1536], replicated, may hold values from 0.1 to 1.9
- wq: bfloat16 [1536, 1024], P('pr', 'tp'), as said below
- wk: bfloat16 [1536, 1024], P('pr', 'tp'), as said below
- wv: bfloat16 [1536, 1536], P('pr', 'tp'), may hold values from -0.3125 to 0.3125
- wo: bfloat16 [1536, 1536], P('tp', 'pr'), may hold values from -0.15625 to 0.15625
- pair_w: bfloat16 [1536, 256], P('tp'), may hold values from -0.3125 to 0.3125
- pair_in: bfloat16 [128, 64, 128], P(('grp', 'seq', 'tp'), 'pr'), parts along dimension 0, may hold values from -6 to 6
- pair_gain: float32 [128], replicated, may hold values from 0.1 to 1.9
- pair_w1: bfloat16 [128, 256], replicated, may hold values from -0.5 to 0.5
- pair_w2: bfloat16 [256, 128], replicated, may hold values from -0.375 to 0.375
Outputs:
- trunk: bfloat16 [2048, 1536], P(('grp', 'seq', 'pr'), 'tp'), parts along dimension 0
- pair_out: bfloat16 [128, 64, 128], P(('grp', 'seq', 'tp'), 'pr'), parts along dimension 0
There are 2 independent parts, one for each index of `grp`. A program takes and returns all parts, laid end to end along the dimension named above; an argument that names none is the same for every part. Nothing has to cross between parts.
Inputs may be any that keep to these rules, and one draw needn't show every extreme that they name: `wq`: before rounding to bfloat16, entries lie between -3.5 / sqrt(1536) and 3.5 / sqrt(1536). `wk`: before rounding to bfloat16, entries lie between -8.75 / sqrt(1536) and 8.75 / sqrt(1536).
All inputs are finite; a program needn't handle non-finite values.
Results may differ from a plain program's by a relative error of at most 0.013.
The roundings to bfloat16 on the way count: a program that leaves them out, or rounds other values in their place, can miss the bound.
Values may be sent and summed in bfloat16 or wider, within the bound.
A program may use at most 64 MiB of HBM per device.

v0:
```python
import math

import jax
import jax.numpy as jnp
from jax import lax
from jax.sharding import PartitionSpec as P

QK = 128
HV = 192
POOL = 16


EPSILON = 1e-06


def extended(value, sides, width):
    for axis, dim in sides:
        devices, length = (lax.axis_size(axis), value.shape[dim])
        up = [(i, (i + 1) % devices) for i in range(devices - 1)]
        down = [(j, i) for i, j in up]
        last = lax.slice_in_dim(value, length - width, length, axis=dim)
        first = lax.slice_in_dim(value, 0, width, axis=dim)
        before = lax.ppermute(last, axis, up)
        after = lax.ppermute(first, axis, down)
        value = jnp.concatenate([before, value, after], axis=dim)
    return value


def rms_scale(values):
    return lax.rsqrt(jnp.mean(values * values, axis=-1, keepdims=True) + EPSILON)


def attention_start(query_block):
    head_count = query_block.shape[1]
    row_count = query_block.shape[0]
    highest = jnp.full((head_count, row_count), -1e30, jnp.float32)
    totals = jnp.zeros((head_count, row_count), jnp.float32)
    mixed = jnp.zeros((row_count, head_count, HV), jnp.float32)
    return (highest, totals, mixed)


def attention_step(query_block, carry, pieces):
    factor = 1.0 / math.sqrt(QK)
    highest, totals, mixed = carry
    key_piece, value_piece = pieces
    scores = (
        jnp.einsum("qhd,khd->hqk", query_block, key_piece, preferred_element_type=jnp.float32)
        * factor
    )
    new_high = jnp.maximum(highest, jnp.max(scores, axis=-1))
    weights = jnp.exp(scores - new_high[:, :, None])
    totals = jnp.sum(weights, axis=-1)
    added = jnp.einsum(
        "hqk,khd->qhd",
        weights.astype(jnp.bfloat16),
        value_piece,
        preferred_element_type=jnp.float32,
    )
    mixed = added
    return (new_high, totals, mixed)


def attention_finish(carry):
    highest, totals, mixed = carry
    return (mixed / jnp.transpose(totals)[:, :, None]).astype(jnp.bfloat16)


def local(
    dna_feats,
    conv_w,
    conv_gain,
    attn_gain,
    wq,
    wk,
    wv,
    wo,
    pair_w,
    pair_in,
    pair_gain,
    pair_w1,
    pair_w2,
):
    row_count = dna_feats.shape[0]
    reach = conv_w.shape[0] // 2
    rimmed = extended(dna_feats, ((("seq", "pr"), 0),), reach)
    channels = lax.all_gather(rimmed, "tp", axis=1, tiled=True)
    conv_empty = jnp.zeros((row_count, conv_w.shape[2]), jnp.float32)
    total = conv_empty
    piece = lax.all_gather(conv_w, "pr", axis=1, tiled=True)
    sliced = channels
    for offset in range(piece.shape[0]):
        total = total + jnp.dot(
            sliced[offset : offset + row_count], piece[offset], preferred_element_type=jnp.float32
        )
    squares = lax.psum(jnp.sum(total * total, axis=1, keepdims=True), "tp")
    model_width = total.shape[1] * lax.axis_size("tp")
    hidden_conv = jax.nn.gelu(
        total * lax.rsqrt(squares / model_width + EPSILON) * conv_gain
    ).astype(jnp.bfloat16)
    trunk_full = lax.all_gather(hidden_conv, "tp", axis=1, tiled=True)
    trunk_wide = trunk_full.astype(jnp.float32)
    normed = (trunk_wide * rms_scale(trunk_wide) * attn_gain).astype(jnp.bfloat16)
    query_width = wq.shape[1]
    pieces = (
        lax.all_gather(wq, "pr", axis=0, tiled=True),
        lax.all_gather(wk, "pr", axis=0, tiled=True),
        lax.all_gather(wv, "pr", axis=0, tiled=True),
    )
    sliced = normed
    query_sum, key_sum, value_sum = tuple(
        (jnp.dot(sliced, piece, preferred_element_type=jnp.float32) for piece in pieces)
    )
    head_count = query_width // QK
    queries = query_sum.astype(jnp.bfloat16).reshape(row_count, head_count, QK)
    keys_local = key_sum.astype(jnp.bfloat16).reshape(row_count, head_count, QK)
    values_local = value_sum.astype(jnp.bfloat16).reshape(row_count, head_count, HV)
    moved_query, moved_keys, moved_values = (
        lax.all_to_all(queries, "pr", split_axis=1, concat_axis=0, tiled=True),
        lax.all_to_all(keys_local, "pr", split_axis=1, concat_axis=0, tiled=True),
        lax.all_to_all(values_local, "pr", split_axis=1, concat_axis=0, tiled=True),
    )
    carried = attention_step(
        moved_query,
        attention_start(moved_query),
        (
            lax.all_gather(moved_keys, "seq", axis=0, tiled=True),
            lax.all_gather(moved_values, "seq", axis=0, tiled=True),
        ),
    )
    attended = lax.all_to_all(
        attention_finish(carried), "pr", split_axis=0, concat_axis=1, tiled=True
    )
    attended_flat = attended.reshape(row_count, head_count * HV)
    head_terms = jnp.dot(
        attended_flat,
        lax.all_gather(wo, "pr", axis=1, tiled=True),
        preferred_element_type=jnp.float32,
    )
    own_share = lax.psum_scatter(
        head_terms.astype(jnp.bfloat16), "tp", scatter_dimension=1, tiled=True
    ).astype(jnp.float32)
    trunk = (hidden_conv.astype(jnp.float32) + own_share).astype(jnp.bfloat16)
    pooled = trunk.astype(jnp.float32).reshape(row_count // POOL, POOL, -1).mean(axis=1)
    partial_embed = jnp.dot(pooled, pair_w.astype(jnp.float32), precision=lax.Precision.HIGHEST)
    embedded = lax.psum(partial_embed, "tp").astype(jnp.bfloat16)
    every_embed = lax.all_gather(embedded, ("seq", "pr"), axis=0, tiled=True)
    pair_rows = pair_in.shape[0]
    pair_cols = pair_in.shape[1]
    pair_width = pair_in.shape[2]
    row_first = lax.axis_index(("seq", "tp")) * pair_rows
    col_first = lax.axis_index("pr") * pair_cols
    row_embed = lax.dynamic_slice_in_dim(every_embed, row_first, pair_rows, 0)[
        :, :pair_width
    ].astype(jnp.float32)
    col_embed = lax.dynamic_slice_in_dim(every_embed, col_first, pair_cols, 0)[
        :, pair_width:
    ].astype(jnp.float32)
    summed = pair_in.astype(jnp.float32) + row_embed[:, None, :] + col_embed[None, :, :]
    pair_normed = (summed * rms_scale(summed) * pair_gain).astype(jnp.bfloat16)
    inner = jax.nn.gelu(
        jnp.dot(pair_normed.reshape(-1, pair_width), pair_w1, preferred_element_type=jnp.float32)
    ).astype(jnp.bfloat16)
    update = jnp.dot(inner, pair_w2, preferred_element_type=jnp.float32).reshape(summed.shape)
    pair_out = (summed + update).astype(jnp.bfloat16)
    return (trunk, pair_out)


def solution(mesh):
    in_specs = (
        P(("grp", "seq", "pr"), "tp"),
        P(None, "pr", "tp"),
        P("tp"),
        P(),
        P("pr", "tp"),
        P("pr", "tp"),
        P("pr", "tp"),
        P("tp", "pr"),
        P("tp", None),
        P(("grp", "seq", "tp"), "pr", None),
        P(),
        P(),
        P(),
    )
    out_specs = (P(("grp", "seq", "pr"), "tp"), P(("grp", "seq", "tp"), "pr", None))
    return jax.shard_map(local, mesh=mesh, in_specs=in_specs, out_specs=out_specs, check_vma=False)
```

profile of v0, /device:TPU:1, one launch (start us, length us, event | category | flops | bytes accessed | tf_op | source)
XLA Modules:
  0.0 160.0 jit_solution(4517351203953663694)
XLA Ops:
  7.2 0.0 copy-start
  7.2 0.0 all-gather.6.cloned.1.call-start
  7.2 0.7 all-gather.6.cloned.1.call-update
  7.9 0.0 all-gather.12.cloned.1.call-start
  8.0 0.7 all-gather.12.cloned.1.call-update
  8.7 0.0 all-gather.10.cloned.1.call-start
  8.7 0.7 all-gather.10.cloned.1.call-update
  9.4 0.0 all-gather.8.cloned.1.call-start
  9.5 0.5 all-gather.8.cloned.1.call-update
  10.0 0.0 all-gather.14.cloned.1.call-start
  10.1 4.6 %collective-permute-start = (bf16[2,384]{1,0:T(2,128)(2,1)S(1)}, bf16[2,384]{1,0:T(2,128)(2,1)S(1)}, u32[]{:S(2)}, u32[]{:S(2)}) collective-permute-start(bf16[2,384]{1,0:T(2,128)(2,1)S(1)} %get-tuple-element.4), channel_id=1, source_target_pairs={{0,1},{1,4},{4,5},{5,8},{8,9},{9,12},{12,13},{2,3},{3,6},{6,7},{7,... | collective-permute-start | bytes 4616 | tf_op jit(solution)/shard_map/ppermute | solution.py:23
  14.6 1.9 %collective-permute-start.1 = (bf16[2,384]{1,0:T(2,128)(2,1)S(1)}, bf16[2,384]{1,0:T(2,128)(2,1)S(1)}, u32[]{:S(2)}, u32[]{:S(2)}) collective-permute-start(bf16[2,384]{1,0:T(2,128)(2,1)S(1)} %get-tuple-element.5), channel_id=1, source_target_pairs={{1,0},{4,1},{5,4},{8,5},{9,8},{12,9},{13,12},{3,2},{6,3},{7,6},{10... | collective-permute-start | bytes 4616 | tf_op jit(solution)/shard_map/ppermute | solution.py:24
  16.6 0.0 all-gather.14.cloned.1.call-update
  16.6 0.0 reduce-scatter.2.cloned.1.call-start
  16.6 0.0 collective-permute-done
  16.7 2.9 %collective-permute-done.1 = bf16[2,384]{1,0:T(2,128)(2,1)S(1)} collective-permute-done((bf16[2,384]{1,0:T(2,128)(2,1)S(1)}, bf16[2,384]{1,0:T(2,128)(2,1)S(1)}, u32[]{:S(2)}, u32[]{:S(2)}) %collective-permute-start.1) | collective-permute-done | bytes 1568 | tf_op jit(solution)/shard_map/ppermute | solution.py:24
  19.6 4.2 %all_gather.30 = bf16[132,768]{1,0:T(8,128)(2,1)S(1)} all-gather(bf16[132,384]{1,0:T(8,128)(2,1)S(1)} %pad_maximum_fusion), channel_id=1, replica_groups=mesh['grp'=2,'seq'=4,'tp'=2,'pr'=2] {'tp'}, dimensions={1}, use_global_device_ids=true | all-gather | bytes 304128 | tf_op jit(solution)/shard_map/all_gather | solution.py:86
  23.8 4.4 %all-gather.6.cloned.1.call-done = bf16[5,768,768]{2,1,0:T(8,128)(2,1)} async-done(((bf16[5,384,768]{2,1,0:T(8,128)(2,1)}), bf16[5,768,768]{2,1,0:T(8,128)(2,1)}) %all-gather.6.cloned.1.call-update) | async-done | bytes 5898256 | tf_op jit(solution)/shard_map/all_gather | solution.py:89
  28.2 1.6 fusion.3
  29.8 1.6 convolution_add_fusion.3
  31.4 1.6 convolution_add_fusion.2
  33.0 0.0 copy-start.4
  33.0 1.6 convolution_add_fusion.1
  34.6 0.0 copy-start.3
  34.6 1.7 %multiply_reduce_fusion.1 = (f32[128]{0:T(128)S(1)}, f32[128,768]{1,0:T(8,128)S(1)}) fusion(f32[128,768]{1,0:T(8,128)S(1)} %convolution_add_fusion.1, bf16[5,768,768]{2,1,0:T(8,128)(2,1)} %all-gather.6.cloned.1.call-done, bf16[132,768]{1,0:T(8,128)(2,1)S(1)} %all_gather.30), kind=kOutput, calls=%fused_computation.42 | convolution fusion | flops 151289728 | bytes 2163200 | tf_op jit(solution)/shard_map/dot_general | solution.py:92
  36.3 3.8 %psum.14 = f32[128,1]{0,1:T(1,128)S(1)} all-reduce(f32[128,1]{0,1:T(1,128)S(1)} %bitcast.89), channel_id=1, replica_groups=mesh['grp'=2,'seq'=4,'tp'=2,'pr'=2] {'tp'}, use_global_device_ids=true, to_apply=%region_1.0 | all-reduce | flops 128 | bytes 1024 | tf_op jit(solution)/shard_map/psum | solution.py:95
  40.2 0.2 fusion.20
  40.4 5.7 %all_gather.32 = bf16[128,1536]{1,0:T(8,128)(2,1)S(1)} all-gather(bf16[128,768]{1,0:T(8,128)(2,1)S(1)} %fusion.20), channel_id=1, replica_groups=mesh['grp'=2,'seq'=4,'tp'=2,'pr'=2] {'tp'}, dimensions={1}, use_global_device_ids=true | all-gather | bytes 589824 | tf_op jit(solution)/shard_map/all_gather | solution.py:100
  46.2 0.2 fusion.10
  46.3 0.0 all-gather.12.cloned.1.call-done
  46.4 1.8 %fusion.6 = bf16[16,4,8,128]{3,2,1,0:T(8,128)(2,1)S(1)} fusion(bf16[1536,512]{1,0:T(8,128)(2,1)} %all-gather.12.cloned.1.call-done, bf16[128,1536]{1,0:T(8,128)(2,1)S(1)} %all_gather.32, f32[1536]{0:T(1024)S(1)} %copy-done.3, f32[128]{0:T(128)S(1)} %add_rsqrt_fusion.1), kind=kOutput, calls=%fused_computation.22 | convolution fusion | flops 202178560 | bytes 2103808 | tf_op jit(solution)/shard_map/dot_general | solution.py:111
  48.3 5.8 %all_to_all.69 = bf16[128,4,128]{2,0,1:T(8,128)(2,1)S(1)} all-to-all(bf16[128,4,128]{2,0,1:T(8,128)(2,1)S(1)} %bitcast.82), channel_id=1, replica_groups=mesh['grp'=2,'seq'=4,'tp'=2,'pr'=2] {'pr'}, dimensions={1} | all-to-all | bytes 262144 | tf_op jit(solution)/shard_map/all_to_all | solution.py:119
  54.1 0.0 all-gather.10.cloned.1.call-done
  54.1 1.8 %fusion.5 = bf16[16,4,8,128]{3,2,1,0:T(8,128)(2,1)S(1)} fusion(bf16[1536,512]{1,0:T(8,128)(2,1)} %all-gather.10.cloned.1.call-done, bf16[128,1536]{1,0:T(8,128)(2,1)S(1)} %all_gather.32, f32[1536]{0:T(1024)S(1)} %copy-done.3, f32[128]{0:T(128)S(1)} %add_rsqrt_fusion.1), kind=kOutput, calls=%fused_computation.21 | convolution fusion | flops 202178560 | bytes 2103808 | tf_op jit(solution)/shard_map/dot_general | solution.py:111
  56.0 3.8 %all_to_all.70 = bf16[128,4,128]{2,0,1:T(8,128)(2,1)S(1)} all-to-all(bf16[128,4,128]{2,0,1:T(8,128)(2,1)S(1)} %bitcast.84), channel_id=1, replica_groups=mesh['grp'=2,'seq'=4,'tp'=2,'pr'=2] {'pr'}, dimensions={1} | all-to-all | bytes 262144 | tf_op jit(solution)/shard_map/all_to_all | solution.py:118
  59.9 7.0 %all-gather.8.cloned.1.call-done = bf16[1536,768]{1,0:T(8,128)(2,1)} async-done(((bf16[768,768]{1,0:T(8,128)(2,1)}), bf16[1536,768]{1,0:T(8,128)(2,1)}) %all-gather.8.cloned.1.call-update) | async-done | bytes 2359312 | tf_op jit(solution)/shard_map/all_gather | solution.py:107
  66.9 2.2 %convolution_convert_fusion.1 = bf16[128,768]{1,0:T(8,128)(2,1)S(1)} fusion(bf16[1536,768]{1,0:T(8,128)(2,1)} %all-gather.8.cloned.1.call-done, bf16[128,1536]{1,0:T(8,128)(2,1)S(1)} %all_gather.32, f32[1536]{0:T(1024)S(1)} %copy-done.3, f32[128]{0:T(128)S(1)} %add_rsqrt_fusion.1), kind=kOutput, calls=%fused_computation.18 | convolution fusion | flops 302874624 | bytes 2955776 | tf_op jit(solution)/shard_map/dot_general | solution.py:111
  69.1 0.2 copy.30
  69.2 3.8 %all_to_all.71 = bf16[128,4,192]{0,2,1:T(8,128)(2,1)S(1)} all-to-all(bf16[128,4,192]{0,2,1:T(8,128)(2,1)S(1)} %bitcast.77), channel_id=1, replica_groups=mesh['grp'=2,'seq'=4,'tp'=2,'pr'=2] {'pr'}, dimensions={1} | all-to-all | bytes 393216 | tf_op jit(solution)/shard_map/all_to_all | solution.py:120
  73.1 14.7 %all_gather.37 = bf16[1024,2,128]{2,0,1:T(8,128)(2,1)S(1)} all-gather(bf16[256,2,128]{2,0,1:T(8,128)(2,1)S(1)} %bitcast.80), channel_id=1, replica_groups=mesh['grp'=2,'seq'=4,'tp'=2,'pr'=2] {'seq'}, dimensions={0}, use_global_device_ids=true | all-gather | bytes 655360 | tf_op jit(solution)/shard_map/all_gather | solution.py:126
  87.8 0.5 multiply_reduce_fusion
  88.4 0.5 fusion
  88.9 14.2 %all_gather.34 = bf16[1024,2,192]{0,2,1:T(8,128)(2,1)S(1)} all-gather(bf16[256,2,192]{0,2,1:T(8,128)(2,1)S(1)} %bitcast.79), channel_id=1, replica_groups=mesh['grp'=2,'seq'=4,'tp'=2,'pr'=2] {'seq'}, dimensions={0}, use_global_device_ids=true | all-gather | bytes 983040 | tf_op jit(solution)/shard_map/all_gather | solution.py:127
  103.1 0.6 fusion.4
  103.7 0.2 copy.36
  103.9 10.0 %all_to_all.72 = bf16[256,2,192]{2,1,0:T(2,128)(2,1)S(1)} all-to-all(bf16[256,2,192]{2,1,0:T(2,128)(2,1)S(1)} %copy.36), channel_id=1, replica_groups=mesh['grp'=2,'seq'=4,'tp'=2,'pr'=2] {'pr'}, dimensions={0} | all-to-all | bytes 393216 | tf_op jit(solution)/shard_map/all_to_all | solution.py:130
  113.9 0.2 copy.38
  114.1 0.0 all-gather.14.cloned.1.call-done
  114.2 0.0 copy-start.1
  114.2 0.0 copy-start.5
  114.2 0.0 copy-start.6
  114.2 0.0 copy-start.7
  114.2 3.0 %convolution_convert_fusion = bf16[128,1536]{1,0:T(8,128)(2,1)} fusion(bf16[128,768]{0,1:T(8,128)(2,1)S(1)} %bitcast.76, bf16[768,1536]{1,0:T(8,128)(2,1)} %all-gather.14.cloned.1.call-done), kind=kOutput, calls=%fused_computation | convolution fusion | flops 302186496 | bytes 2949120 | tf_op jit(solution)/shard_map/dot_general | solution.py:134
  117.2 0.0 reduce-scatter.2.cloned.1.call-update
  117.2 12.7 %reduce-scatter.2.cloned.1.call-done = bf16[128,768]{1,0:T(8,128)(2,1)} async-done(((bf16[128,1536]{1,0:T(8,128)(2,1)}), bf16[128,768]{1,0:T(8,128)(2,1)}) %reduce-scatter.2.cloned.1.call-update) | async-done | bytes 196624 | tf_op jit(solution)/shard_map/reduce_scatter | solution.py:139
  129.9 1.9 %convert_reduce_fusion = (f32[8,768]{1,0:T(8,128)S(1)}, bf16[128,768]{1,0:T(8,128)(2,1)}) fusion(bf16[128,768]{1,0:T(8,128)(2,1)} %reduce-scatter.2.cloned.1.call-done, f32[768]{0:T(1024)S(1)} %copy-done.4, f32[128,768]{1,0:T(8,128)S(1)} %get-tuple-element.7, f32[128]{0:T(128)S(1)} %rsqrt_bitcast_fusion), kind=kLoop, calls=%fused_computation.39 | loop fusion | flops 1665024 | bytes 814592 | tf_op jit(solution)/shard_map/reduce_sum | solution.py:143
  131.8 0.2 fusion.39
  132.1 3.9 %psum.15 = bf16[8,256]{1,0:T(8,128)(2,1)S(1)} all-reduce(f32[8,256]{1,0:T(8,128)S(1)} %fusion.39), channel_id=1, replica_groups=mesh['grp'=2,'seq'=4,'tp'=2,'pr'=2] {'tp'}, use_global_device_ids=true, to_apply=%region_7.0 | all-reduce | flops 2048 | bytes 12288 | tf_op jit(solution)/shard_map/psum | solution.py:145
  135.9 16.0 %all_gather.39 = bf16[64,256]{1,0:T(8,128)(2,1)S(1)} all-gather(bf16[8,256]{1,0:T(8,128)(2,1)S(1)} %psum.15), channel_id=1, replica_groups=mesh['grp'=2,'seq'=4,'tp'=2,'pr'=2] {'seq','pr'}, dimensions={0}, use_global_device_ids=true | all-gather | bytes 36864 | tf_op jit(solution)/shard_map/all_gather | solution.py:146
  151.9 0.0 copy-done.1
  151.9 0.1 multiply_reduce_fusion.2
  152.0 0.1 multiply_convert_fusion
  152.2 0.3 fusion.29
  152.5 0.7 add_convert_fusion.1
  (21 shorter events, 0.2 us)
Async XLA Ops:
  7.2 124.6 %copy-start = (bf16[768,256]{1,0:T(8,128)(2,1)S(1)}, bf16[768,256]{1,0:T(8,128)(2,1)}, u32[]{:S(2)}) copy-start(bf16[768,256]{1,0:T(8,128)(2,1)} %param.21) | copy-start | bytes 1179652
  7.2 21.0 %all-gather.6.cloned.1.call-start = ((), (), s32[]{:S(2)}) async-start(), calls=%async_computation.5 | async-start | bytes 8847360 | tf_op jit(solution)/shard_map/all_gather | solution.py:89
  7.9 2.1 %copy-start.2 = (bf16[128,384]{1,0:T(8,128)(2,1)S(1)}, bf16[128,384]{1,0:T(8,128)(2,1)}, u32[]{:S(2)}) copy-start(bf16[128,384]{1,0:T(8,128)(2,1)} %param.13) | copy-start | bytes 294916
  7.9 38.4 %all-gather.12.cloned.1.call-start = ((), (), s32[]{:S(2)}) async-start(), calls=%async_computation.8 | async-start | bytes 2359296 | tf_op jit(solution)/shard_map/all_gather | solution.py:106
  8.7 45.5 %all-gather.10.cloned.1.call-start = ((), (), s32[]{:S(2)}) async-start(), calls=%async_computation.7 | async-start | bytes 2359296 | tf_op jit(solution)/shard_map/all_gather | solution.py:105
  9.4 57.5 %all-gather.8.cloned.1.call-start = ((), (), s32[]{:S(2)}) async-start(), calls=%async_computation.6 | async-start | bytes 3538944 | tf_op jit(solution)/shard_map/all_gather | solution.py:107
  10.0 104.2 %all-gather.14.cloned.1.call-start = ((), (), s32[]{:S(2)}) async-start(), calls=%async_computation.9 | async-start | bytes 3538944 | tf_op jit(solution)/shard_map/all_gather | solution.py:136
  10.1 6.6 %collective-permute-start = (bf16[2,384]{1,0:T(2,128)(2,1)S(1)}, bf16[2,384]{1,0:T(2,128)(2,1)S(1)}, u32[]{:S(2)}, u32[]{:S(2)}) collective-permute-start(bf16[2,384]{1,0:T(2,128)(2,1)S(1)} %get-tuple-element.4), channel_id=1, source_target_pairs={{0,1},{1,4},{4,5},{5,8},{8,9},{9,12},{12,13},{2,3},{3,6},{6,7},{7,... | collective-permute-start | bytes 4616 | tf_op jit(solution)/shard_map/ppermute | solution.py:23
  14.6 4.9 %collective-permute-start.1 = (bf16[2,384]{1,0:T(2,128)(2,1)S(1)}, bf16[2,384]{1,0:T(2,128)(2,1)S(1)}, u32[]{:S(2)}, u32[]{:S(2)}) collective-permute-start(bf16[2,384]{1,0:T(2,128)(2,1)S(1)} %get-tuple-element.5), channel_id=1, source_target_pairs={{1,0},{4,1},{5,4},{8,5},{9,8},{12,9},{13,12},{3,2},{6,3},{7,6},{10... | collective-permute-start | bytes 4616 | tf_op jit(solution)/shard_map/ppermute | solution.py:24
  16.6 113.3 %reduce-scatter.2.cloned.1.call-start = ((), (), s32[]{:S(2)}) async-start(), calls=%async_computation.10 | async-start | bytes 589824 | tf_op jit(solution)/shard_map/reduce_scatter | solution.py:139
  33.0 7.2 %copy-start.4 = (f32[768]{0:T(1024)S(1)}, f32[768]{0:T(1024)}, u32[]{:S(2)}) copy-start(f32[768]{0:T(1024)} %param.15) | copy-start | bytes 9220
  34.6 11.7 %copy-start.3 = (f32[1536]{0:T(1024)S(1)}, f32[1536]{0:T(1024)}, u32[]{:S(2)}) copy-start(f32[1536]{0:T(1024)} %param.16) | copy-start | bytes 18436
  114.2 37.7 %copy-start.1 = (bf16[8,32,128]{2,1,0:T(8,128)(2,1)S(1)}, bf16[8,32,128]{2,1,0:T(8,128)(2,1)}, u32[]{:S(2)}) copy-start(bf16[8,32,128]{2,1,0:T(8,128)(2,1)} %param.22) | copy-start | bytes 196612
  114.2 37.9 %copy-start.5 = (f32[128]{0:T(128)S(1)}, f32[128]{0:T(128)}, u32[]{:S(2)}) copy-start(f32[128]{0:T(128)} %param.23) | copy-start | bytes 1540
  114.2 38.0 %copy-start.6 = (bf16[256,128]{1,0:T(8,128)(2,1)S(1)}, bf16[256,128]{1,0:T(8,128)(2,1)}, u32[]{:S(2)}) copy-start(bf16[256,128]{1,0:T(8,128)(2,1)} %param.25) | copy-start | bytes 196612
  114.2 38.0 %copy-start.7 = (bf16[128,256]{1,0:T(8,128)(2,1)S(1)}, bf16[128,256]{1,0:T(8,128)(2,1)}, u32[]{:S(2)}) copy-start(bf16[128,256]{1,0:T(8,128)(2,1)} %param.24) | copy-start | bytes 196612
Sparse Core Ops, SparseCore 0:
  9.5 18.6 all-gather.5
  29.7 10.9 all-gather.11
  42.3 10.9 all-gather.9
  54.7 12.1 all-gather.7
  68.3 12.1 all-gather.13
  117.3 12.5 reduce-scatter.1
where the time goes:
time: 161 us; the launch traced here: 160 us
  blocking collectives  86.1 us (53%)
  waiting for transfers between devices  29.7 us (18%)
  matrix products  18.6 us (12%)
  between operations  14.4 us (9%)
  starting transfers between devices  6.73 us (4%)
  other arithmetic  3.73 us (2%)
    all_gather x1, blocking collectives, local(): every_embed = lax.all_gather(embedded, ('seq', 'pr'), axis=0, tiled=True)  16 us
    all_gather x1, blocking collectives, local(): lax.all_gather(moved_keys, 'seq', axis=0, tiled=True)  14.7 us
    all_gather x1, blocking collectives, local(): lax.all_gather(moved_values, 'seq', axis=0, tiled=True)  14.2 us
    reduce_scatter x1, waiting for transfers between devices, local(): lax.psum_scatter(head_terms.astype(jnp.bfloat16), 'tp', scatter_dimension...  12.7 us
    all_to_all x1, blocking collectives, local(): lax.all_to_all(attention_finish(carried), 'pr', split_axis=0, concat_axis...  10 us
    dot_general x5, matrix products, local(): jnp.dot(sliced[offset:offset + row_count], piece[offset], preferred_eleme...  8.08 us
    all_gather x1, waiting for transfers between devices, local(): lax.all_gather(wv, 'pr', axis=0, tiled=True)  7.01 us
    all_to_all x1, blocking collectives, local(): lax.all_to_all(keys_local, 'pr', split_axis=1, concat_axis=0, tiled=True)  5.85 us
  transfers between devices with their start and end apart: 8, of which 4 were waited for; matrix products, arithmetic and copies ran while one was open for 10% of the time, Pallas kernels for 0%

commit v1 on v0

--- a/solution.py
+++ b/solution.py
@@ -3,6 +3,8 @@
 import jax
 import jax.numpy as jnp
 from jax import lax
+from jax.experimental import pallas as pl
+from jax.experimental.pallas import tpu as pltpu
 from jax.sharding import PartitionSpec as P
 
 QK = 128
@@ -165,6 +167,397 @@
     return (trunk, pair_out)
 
 
+def gelu_tanh(x):
+    return 0.5 * x * (1.0 + jnp.tanh(math.sqrt(2.0 / math.pi) * (x + 0.044715 * (x * x * x))))
+
+
+def to_rows(column):
+    rows = column.shape[0]
+    return jnp.transpose(jnp.broadcast_to(column, (rows, 128)))[:8]
+
+
+def to_column(tile):
+    rows = tile.shape[1]
+    return jnp.transpose(jnp.broadcast_to(tile[:1], (128, rows)))[:, :1]
+
+
+class Sems:
+    def __init__(self, ref, limit):
+        self.ref, self.limit, self.used = ref, limit, 0
+
+    def take(self, count=1):
+        first = self.used
+        self.used += count
+        assert self.used <= self.limit
+        return first
+
+
+SENDS = 96
+RECVS = 96
+HALO = 16
+
+
+def fused_kernel(
+    x_ref, cw_hbm, cg_ref, ag_ref, wq_hbm, wk_hbm, wv_hbm, wo_hbm, pw_hbm, pin_ref, pg_ref, w1_ref, w2_ref,
+    trunk_ref, pout_ref,
+    cw, wq, wk, wv, wo, pw,
+    xin, xf, im, acc, accr, q1, q1r, hid, hall, s2, nrm, part, partr,
+    qo, ko, vo, qb, kb, vb, ao, at, ot, tin, eb, rowb, colb,
+    lsem, ssem, rsem,
+):
+    s, t, p = lax.axis_index("seq"), lax.axis_index("tp"), lax.axis_index("pr")
+    n_seq = lax.axis_size("seq")
+    rows = x_ref.shape[0]
+    cin = x_ref.shape[1]
+    half = hid.shape[1]
+    width = 2 * half
+    sends, recvs = Sems(ssem, SENDS), Sems(rsem, RECVS)
+    pending = []
+    f32, bf16 = jnp.float32, jnp.bfloat16
+
+    def remote(src, dst, recv, dev, cond=None):
+        copy = pltpu.make_async_remote_copy(
+            src_ref=src, dst_ref=dst, send_sem=ssem.at[sends.take()], recv_sem=rsem.at[recv],
+            device_id=dev, device_id_type=pl.DeviceIdType.MESH,
+        )
+        if cond is None:
+            copy.start()
+        else:
+            pl.when(cond)(lambda: copy.start())
+        pending.append((copy, cond))
+
+    def arrived(dst, recv, cond=None):
+        copy = pltpu.make_async_remote_copy(
+            src_ref=dst, dst_ref=dst, send_sem=ssem.at[0], recv_sem=rsem.at[recv],
+            device_id={"pr": 1 - p}, device_id_type=pl.DeviceIdType.MESH,
+        )
+        if cond is None:
+            copy.wait_recv()
+        else:
+            pl.when(cond)(lambda: copy.wait_recv())
+
+    loads = [pltpu.make_async_copy(a, b, lsem.at[i]) for i, (a, b) in enumerate(
+        ((cw_hbm, cw), (wq_hbm, wq), (wk_hbm, wk), (wv_hbm, wv), (wo_hbm, wo), (pw_hbm, pw)))]
+    for load in loads:
+        load.start()
+
+    barrier = pltpu.get_barrier_semaphore()
+    for ds in range(n_seq):
+        for dt in range(2):
+            for dp in range(2):
+                if ds or dt or dp:
+                    pl.semaphore_signal(
+                        barrier, inc=1,
+                        device_id={"seq": lax.rem(s + ds, n_seq), "tp": lax.rem(t + dt, 2), "pr": lax.rem(p + dp, 2)},
+                        device_id_type=pl.DeviceIdType.MESH)
+    pl.semaphore_wait(barrier, 4 * n_seq - 1)
+
+    other_t, other_p = 1 - t, 1 - p
+    diag = p == t
+    off = p != t
+
+    r_x = recvs.take(4)
+    mine = pl.ds(pl.multiple_of(HALO + p * rows, HALO), rows)
+    for td in (other_t, t):
+        low, high = xin.at[pl.ds(0, HALO)], xin.at[pl.ds(HALO + 2 * rows, HALO)]
+        remote(x_ref, xin.at[mine], r_x + p, {"tp": td, "pr": t}, None if td is other_t else off)
+        remote(x_ref.at[pl.ds(rows - HALO, HALO)], low, r_x + 2,
+               {"seq": lax.rem(s + 1, n_seq), "tp": td, "pr": t}, (p == 1) & (s < n_seq - 1))
+        remote(x_ref.at[pl.ds(0, HALO)], high, r_x + 3,
+               {"seq": lax.rem(s + n_seq - 1, n_seq), "tp": td, "pr": t}, (p == 0) & (s > 0))
+
+    @pl.when(diag)
+    def _():
+        xin[mine, :] = x_ref[...]
+
+    @pl.when(s == 0)
+    def _():
+        xin[pl.ds(0, HALO), :] = jnp.zeros((HALO, cin), bf16)
+
+    @pl.when(s == n_seq - 1)
+    def _():
+        xin[pl.ds(HALO + 2 * rows, HALO), :] = jnp.zeros((HALO, cin), bf16)
+
+    for q in range(2):
+        arrived(xin.at[pl.ds(HALO + q * rows, rows)], r_x + q, off | (p != q))
+    arrived(xin.at[pl.ds(0, HALO)], r_x + 2, s > 0)
+    arrived(xin.at[pl.ds(HALO + 2 * rows, HALO)], r_x + 3, s < n_seq - 1)
+
+    xf[...] = xin[...].astype(f32)
+    taps = im.shape[1] // cin
+    for o in range(taps):
+        im[:, o * cin:(o + 1) * cin] = xf[pl.ds(HALO - taps // 2 + o, 2 * rows), :].astype(bf16)
+
+    own = pl.ds(pl.multiple_of(p * rows, rows), rows)
+    theirs = pl.ds(pl.multiple_of(other_p * rows, rows), rows)
+    partner = {"pr": other_p}
+    loads[0].wait()
+    step = 256
+    chunks = half // step
+    r_c = recvs.take(chunks)
+    for c in range(chunks):
+        cols = pl.ds(c * step, step)
+        acc[:, cols] = jnp.dot(im[...], cw[:, cols], preferred_element_type=f32)
+        remote(acc.at[theirs, cols], accr.at[:, cols], r_c + c, partner)
+    square = jnp.zeros((rows, 1), f32)
+    for c in range(chunks):
+        cols = pl.ds(c * step, step)
+        arrived(accr.at[:, cols], r_c + c)
+        value = acc[own, cols] + accr[:, cols]
+        accr[:, cols] = value
+        square = square + jnp.sum(value * value, axis=1, keepdims=True)
+    q1[...] = to_rows(square)
+    r_q = recvs.take()
+    remote(q1, q1r, r_q, {"tp": other_t})
+    arrived(q1r, r_q)
+    scale = to_column(lax.rsqrt((q1[...] + q1r[...]) / width + EPSILON))
+
+    me4 = t * 2 + p
+    r_h = recvs.take(2 * chunks)
+    hmine = own
+    square = jnp.zeros((rows, 1), f32)
+    for c in range(chunks):
+        cols = pl.ds(c * step, step)
+        rounded = gelu_tanh(accr[:, cols] * scale * cg_ref[:, cols]).astype(bf16)
+        hid[:, cols] = rounded
+        wide = rounded.astype(f32)
+        square = square + jnp.sum(wide * wide, axis=1, keepdims=True)
+        remote(hid.at[:, cols], hall.at[hmine, cols], r_h + 2 * c + p, {"tp": other_t, "pr": t})
+        remote(hid.at[:, cols], hall.at[hmine, cols], r_h + 2 * c + p, {"pr": t}, off)
+    s2[me4] = to_rows(square)
+    r_s = recvs.take(4)
+    for dt in range(2):
+        for dp in range(2):
+            if dt or dp:
+                remote(s2.at[me4], s2.at[me4], r_s + me4, {"tp": lax.rem(t + dt, 2), "pr": lax.rem(p + dp, 2)})
+
+    @pl.when(diag)
+    def _():
+        hall[hmine, :] = hid[...]
+
+    for i in range(4):
+        arrived(s2.at[i], r_s + i, me4 != i)
+    for q in range(2):
+        for c in range(chunks):
+            arrived(hall.at[pl.ds(q * rows, rows), pl.ds(c * step, step)], r_h + 2 * c + q, off | (p != q))
+        scale = to_column(lax.rsqrt((s2[q] + s2[2 + q]) / width + EPSILON))
+        block = pl.ds(q * rows, rows)
+        nrm[block, :] = (hall[block, :].astype(f32) * scale * ag_ref[p]).astype(bf16)
+
+    for load in loads[1:]:
+        load.wait()
+    heads = n_seq
+    qk = heads * QK
+    base_k, base_v, base_q = 0, qk, qk + heads * HV
+    plan = [(wk, base_k, c) for c in range(qk // step)] + [
+        (wv, base_v, c) for c in range(heads * HV // step)] + [(wq, base_q, c) for c in range(qk // step)]
+    r_p = recvs.take(len(plan))
+    for i, (w, base, c) in enumerate(plan):
+        cols = pl.ds(base + c * step, step)
+        part[:, cols] = jnp.dot(nrm[...], w[:, c * step:(c + 1) * step], preferred_element_type=f32)
+        remote(part.at[theirs, cols], partr.at[:, cols], r_p + i, partner)
+
+    def finish(i):
+        w, base, c = plan[i]
+        cols = pl.ds(base + c * step, step)
+        arrived(partr.at[:, cols], r_p + i)
+
+    def total(first, count):
+        return (part[own, first:first + count] + partr[:, first:first + count]).astype(bf16)
+
+    far = (2, 1, 3) if n_seq == 4 else tuple(range(1, n_seq))
+
+    def scatter(src, dst_of, recv):
+        for d in far:
+            h = lax.rem(s + d, n_seq)
+            remote(src.at[h], dst_of(s), recv + d, {"seq": h})
+
+    r_k, r_v, r_qq = recvs.take(n_seq), recvs.take(n_seq), recvs.take(n_seq)
+    n_k, n_v = qk // step, heads * HV // step
+    for i in range(n_k):
+        finish(i)
+    for h in range(heads):
+        ko[h] = total(base_k + h * QK, QK)
+    scatter(ko, lambda j: kb.at[j, p], r_k)
+    kb[s, p] = ko[s]
+    for i in range(n_k, n_k + n_v):
+        finish(i)
+    for h in range(heads):
+        vo[h] = total(base_v + h * HV, HV)
+    scatter(vo, lambda j: vb.at[j, p], r_v)
+    vb[s, p] = vo[s]
+    for i in range(n_k + n_v, len(plan)):
+        finish(i)
+    for h in range(heads):
+        qo[h] = total(base_q + h * QK, QK)
+    scatter(qo, lambda j: qb.at[j], r_qq)
+    qb[s] = qo[s]
+
+    r_k2, r_v2 = recvs.take(n_seq), recvs.take(n_seq)
+    near = (0, 1, 3, 2) if n_seq == 4 else tuple(range(n_seq))
+    for buf, got, on in ((kb, r_k, r_k2), (vb, r_v, r_v2)):
+        for d in near:
+            j = lax.rem(s + n_seq - d, n_seq)
+            if d:
+                arrived(buf.at[j, p], got + d)
+            remote(buf.at[j, p], buf.at[j, p], on + d, partner)
+    for buf, on in ((kb, r_k2), (vb, r_v2)):
+        for d in near:
+            j = lax.rem(s + n_seq - d, n_seq)
+            arrived(buf.at[j, other_p], on + d)
+
+    factor = 1.0 / math.sqrt(QK)
+    r_a, r_a2 = recvs.take(n_seq), recvs.take(n_seq)
+    keys_total = 2 * n_seq * rows
+    for d in far + (0,):
+        j = lax.rem(s + n_seq - d, n_seq)
+        if d:
+            arrived(qb.at[j], r_qq + d)
+        scores = lax.dot_general(
+            qb[j], kb[...].reshape(keys_total, QK), (((1,), (1,)), ((), ())), preferred_element_type=f32) * factor
+        weights = jnp.exp(scores - jnp.max(scores, axis=1, keepdims=True))
+        sums = jnp.sum(weights, axis=1, keepdims=True)
+        mixed = jnp.dot(weights.astype(bf16), vb[...].reshape(keys_total, HV), preferred_element_type=f32)
+        result = (mixed / sums).astype(bf16)
+        if d:
+            ao[d] = result
+            remote(ao.at[d], at.at[s, p], r_a + d, {"seq": j})
+        else:
+            at[s, p] = result
+    for d in (0,) + far[::-1]:
+        h = lax.rem(s + d, n_seq)
+        if d:
+            arrived(at.at[h, p], r_a + d)
+        remote(at.at[h, p], at.at[h, p], r_a2 + d, partner)
+    for d in range(n_seq):
+        arrived(at.at[lax.rem(s + d, n_seq), other_p], r_a2 + d)
+
+    r_o = recvs.take(2 * chunks)
+    for c in range(chunks):
+        cols = pl.ds(c * step, step)
+        value = jnp.zeros((2 * rows, step), f32)
+        for h in range(heads):
+            value = value + jnp.dot(
+                at[h].reshape(2 * rows, HV), wo[h * HV:(h + 1) * HV, cols], preferred_element_type=f32)
+        ot[:, cols] = value.astype(bf16)
+        remote(ot.at[theirs, cols], tin.at[t, :, cols], r_o + 2 * c + t, {"tp": p, "pr": other_p})
+        remote(ot.at[own, cols], tin.at[t, :, cols], r_o + 2 * c + t, {"tp": p}, off)
+
+        @pl.when(diag)
+        def _():
+            tin[t, :, cols] = ot[own, cols]
+
+    partial = jnp.zeros((8, 2 * pin_ref.shape[2]), f32)
+    groups = rows // POOL
+    for c in range(chunks):
+        cols = pl.ds(c * step, step)
+        for i in range(2):
+            arrived(tin.at[i, :, cols], r_o + 2 * c + i, off | (t != i))
+        trunk = (hid[:, cols].astype(f32) + (tin[0, :, cols].astype(f32) + tin[1, :, cols].astype(f32))).astype(bf16)
+        trunk_ref[:, cols] = trunk
+        pooled = jnp.sum(trunk.astype(f32).reshape(groups, POOL, step), axis=1) * (1.0 / POOL)
+        first = pooled.astype(bf16)
+        rest = pooled - first.astype(f32)
+        second = rest.astype(bf16)
+        third = (rest - second.astype(f32)).astype(bf16)
+        for piece in (third, second, first):
+            partial = partial + jnp.dot(piece, pw[c * step:(c + 1) * step, :], preferred_element_type=f32)
+    pair = pin_ref.shape[2]
+    eb[0] = partial[:, :pair]
+    eb[1] = partial[:, pair:]
+    r_r, r_e = recvs.take(2), recvs.take(8)
+    remote(eb.at[0], rowb.at[t], r_r + t, {"tp": p, "pr": other_p})
+    remote(eb.at[0], rowb.at[t], r_r + t, {"tp": p}, off)
+
+    @pl.when(diag)
+    def _():
+        rowb[t] = eb[0]
+
+    side = s // 2
+    slot = lax.rem(s, 2) * 2 + p
+    for d in far + (0,):
+        for dt in range(2):
+            remote(eb.at[1], colb.at[t, slot], r_e + t * 4 + slot,
+                   {"seq": lax.rem(s + d, n_seq), "tp": lax.rem(t + dt, 2), "pr": side},
+                   (p != side) if d == 0 and dt == 0 else None)
+
+    @pl.when(p == side)
+    def _():
+        colb[t, slot] = eb[1]
+
+    for i in range(2):
+        arrived(rowb.at[i], r_r + i, off | (t != i))
+    for i in range(2):
+        for k in range(4):
+            arrived(colb.at[i, k], r_e + i * 4 + k, (t != i) | (slot != k) | (p != side))
+    row_embed = (rowb[0] + rowb[1]).astype(bf16).astype(f32)
+    col_embed = (colb[0] + colb[1]).reshape(4 * groups, pair).astype(bf16).astype(f32)
+    summed = pin_ref[...].astype(f32) + row_embed[:, None, :] + col_embed[None, :, :]
+    flat = summed.reshape(-1, pair)
+    inv = lax.rsqrt(jnp.mean(flat * flat, axis=1, keepdims=True) + EPSILON)
+    normal = (flat * inv * pg_ref[...]).astype(bf16)
+    inner = gelu_tanh(jnp.dot(normal, w1_ref[...], preferred_element_type=f32)).astype(bf16)
+    update = jnp.dot(inner, w2_ref[...], preferred_element_type=f32)
+    pout_ref[...] = (flat + update).astype(bf16).reshape(pout_ref.shape)
+
+    for copy, cond in pending:
+        if cond is None:
+            copy.wait_send()
+        else:
+            pl.when(cond)(lambda copy=copy: copy.wait_send())
+
+
+def fused(dna_feats, conv_w, conv_gain, attn_gain, wq, wk, wv, wo, pair_w, pair_in, pair_gain, pair_w1, pair_w2):
+    rows, cin = dna_feats.shape
+    taps, _, half = conv_w.shape
+    heads = lax.axis_size("seq")
+    width = half * 2
+    bf16, f32 = jnp.bfloat16, jnp.float32
+    vmem = pl.BlockSpec(memory_space=pltpu.VMEM)
+    hbm = pl.BlockSpec(memory_space=pl.ANY)
+    flat_conv = conv_w.reshape(taps * cin, half)
+    total = heads * (2 * QK + HV)
+    pair = pair_in.shape[2]
+    groups = rows // POOL
+    v = pltpu.VMEM
+    scratch = [
+        v(flat_conv.shape, bf16), v(wq.shape, bf16), v(wk.shape, bf16), v(wv.shape, bf16), v(wo.shape, bf16),
+        v(pair_w.shape, bf16),
+        v((2 * rows + 2 * HALO, cin), bf16), v((2 * rows + 2 * HALO, cin), f32), v((2 * rows, taps * cin), bf16),
+        v((2 * rows, half), f32), v((rows, half), f32), v((8, rows), f32), v((8, rows), f32),
+        v((rows, half), bf16), v((2 * rows, half), bf16), v((4, 8, rows), f32), v((2 * rows, half), bf16),
+        v((2 * rows, total), f32), v((rows, total), f32),
+        v((heads, rows, QK), bf16), v((heads, rows, QK), bf16), v((heads, rows, HV), bf16),
+        v((heads, rows, QK), bf16), v((heads, 2, rows, QK), bf16), v((heads, 2, rows, HV), bf16),
+        v((heads, rows, HV), bf16), v((heads, 2, rows, HV), bf16),
+        v((2 * rows, half), bf16), v((2, rows, half), bf16),
+        v((2, groups, pair), f32), v((2, groups, pair), f32), v((2, 4, groups, pair), f32),
+        pltpu.SemaphoreType.DMA((8,)), pltpu.SemaphoreType.DMA((SENDS,)), pltpu.SemaphoreType.DMA((RECVS,)),
+    ]
+    return pl.pallas_call(
+        fused_kernel,
+        out_shape=(jax.ShapeDtypeStruct((rows, half), bf16), jax.ShapeDtypeStruct(pair_in.shape, bf16)),
+        in_specs=[vmem, hbm, vmem, vmem, hbm, hbm, hbm, hbm, hbm, vmem, vmem, vmem, vmem],
+        out_specs=(vmem, vmem),
+        scratch_shapes=scratch,
+        compiler_params=pltpu.CompilerParams(
+            collective_id=0, has_side_effects=True, vmem_limit_bytes=60 * 1024 * 1024),
+    )(dna_feats, flat_conv, conv_gain.reshape(1, half), attn_gain.reshape(2, 1, half), wq, wk, wv, wo, pair_w,
+      pair_in, pair_gain.reshape(1, pair), pair_w1, pair_w2)
+
+
+def block(*arrays):
+    dna_feats, conv_w, wq = arrays[0], arrays[1], arrays[4]
+    n_seq, n_tp, n_pr = (lax.axis_size(a) for a in ("seq", "tp", "pr"))
+    fits = (
+        n_tp == 2 and n_pr == 2 and n_seq == 4 and wq.shape[1] == n_seq * QK
+        and dna_feats.shape[0] == 128 and conv_w.shape[1] == dna_feats.shape[1]
+        and arrays[3].shape[0] == 2 * conv_w.shape[2] and conv_w.shape[2] % 256 == 0
+        and arrays[9].shape[0] * POOL == dna_feats.shape[0]
+    )
+    return fused(*arrays) if fits else local(*arrays)
+
+
 def solution(mesh):
     in_specs = (
         P(("grp", "seq", "pr"), "tp"),
@@ -182,4 +575,4 @@
         P(),
     )
     out_specs = (P(("grp", "seq", "pr"), "tp"), P(("grp", "seq", "tp"), "pr", None))
-    return jax.shard_map(local, mesh=mesh, in_specs=in_specs, out_specs=out_specs, check_vma=False)
+    return jax.shard_map(block, mesh=mesh, in_specs=in_specs, out_specs=out_specs, check_vma=False)

time: 161 us -> 67.2 us (0.42)
  blocking collectives: 86.1 us -> 0 us
  Pallas kernels: 0 us -> 60.6 us
  waiting for transfers between devices: 29.7 us -> 0 us
  matrix products: 18.6 us -> 0 us
  between operations: 14.4 us -> 0.64 us
  starting transfers between devices: 6.73 us -> 0 us
  local copies, waits for them, and re-layouts: 0.69 us -> 5.66 us
  other arithmetic: 3.73 us -> 0 us
    pallas_call x0 -> x1, Pallas kernels: none -> 60.6 us  [fused(): pl.pallas_call(fused_kernel, out_shape=(jax.ShapeDtypeStruct((rows, half)...]
    all_gather x5 -> x0, blocking collectives: 54.9 us -> none  [the longest x1 16 us: local(): every_embed = lax.all_gather(embedded, ('seq', 'pr'), axis=0, tiled=True)]
    all_to_all x4 -> x0, blocking collectives: 23.5 us -> none  [the longest x1 10 us: local(): lax.all_to_all(attention_finish(carried), 'pr', split_axis=0, concat_axis...]
    dot_general x13 -> x0, matrix products: 18.6 us -> none  [the longest x5 8.08 us: local(): jnp.dot(sliced[offset:offset + row_count], piece[offset], preferred_eleme...]
    reduce_scatter x1 -> x0, waiting for transfers between devices: 12.7 us -> none  [local(): lax.psum_scatter(head_terms.astype(jnp.bfloat16), 'tp', scatter_dimension...]
    all_gather x5 -> x0, waiting for transfers between devices: 11.5 us -> none  [the longest x1 7.01 us: local(): lax.all_gather(wv, 'pr', axis=0, tiled=True)]
    psum x2 -> x0, blocking collectives: 7.71 us -> none  [the longest x1 3.87 us: local(): embedded = lax.psum(partial_embed, 'tp').astype(jnp.bfloat16)]
    ppermute x2 -> x0, starting transfers between devices: 6.5 us -> none  [the longest x1 4.58 us: extended(): before = lax.ppermute(last, axis, up)]
  transfers between devices with their start and end apart: 8 -> 0, of which waited for: 4 -> 0; matrix products, arithmetic and copies ran while one was open for 10% -> 0% of each run, Pallas kernels for 0% -> 0%
where the time goes in v1:
time: 67.2 us; the launch traced here: 66.9 us
  Pallas kernels  60.6 us (90%)
  local copies, waits for them, and re-layouts  5.66 us (8%)
    pallas_call x1, Pallas kernels, fused(): pl.pallas_call(fused_kernel, out_shape=(jax.ShapeDtypeStruct((rows, half)...  60.6 us
    unnamed x2, local copies, waits for them, and re-layouts  3.09 us

profile of v1, /device:TPU:1, one launch (start us, length us, event | category | flops | bytes accessed | tf_op | source)
XLA Modules:
  0.0 66.9 jit_solution(15772983972467388056)
XLA Ops:
  0.6 1.3 %reshape.17.cg_ref = f32[1,768]{1,0:T(1,128)} reshape(f32[768]{0:T(1024)} %param.15) | data formatting | bytes 6144 | tf_op jit(solution)/shard_map/reshape | solution.py:545
  1.9 1.3 %reshape.18.ag_ref = f32[2,1,768]{2,1,0:T(1,128)} reshape(f32[1536]{0:T(1024)} %param.16) | data formatting | bytes 12288 | tf_op jit(solution)/shard_map/reshape | solution.py:545
  3.2 60.6 %shard_map.140 = (bf16[128,768]{1,0:T(8,128)(2,1)}, bf16[8,32,128]{2,1,0:T(8,128)(2,1)}) custom-call(bf16[128,384]{1,0:T(8,128)(2,1)} %x_ref.1, bf16[1920,768]{1,0:T(8,128)(2,1)} %bitcast.2, f32[1,768]{1,0:T(1,128)} %reshape.17.cg_ref, f32[2,1,768]{2,1,0:T(1,128)} %reshape.18.ag_ref, bf16[768,512]{1,0:T(8,128)(2,1)} %wq_hbm.1, bf16[768,512]{1,0:T(8,128)(2,1)} %wk_hbm.1, ...), custom_call_target="tpu_custom_call" | custom-call | tf_op jit(solution)/shard_map/pallas_call | solution.py:537
  63.8 1.6 %copy.17 = bf16[128,768]{1,0:T(8,128)(2,1)} copy(bf16[128,768]{1,0:T(8,128)(2,1)} %get-tuple-element.4) | data formatting | bytes 393216
  65.4 1.5 %copy.18 = bf16[8,32,128]{2,1,0:T(8,128)(2,1)} copy(bf16[8,32,128]{2,1,0:T(8,128)(2,1)} %get-tuple-element.5) | data formatting | bytes 131072

commit v2 on v1

--- a/solution.py
+++ b/solution.py
@@ -192,6 +192,22 @@
         return first
 
 
+def fold(ref, value):
+    rows, extra = value.shape[0], value.shape[1] - 128
+    ref[pl.ds(0, rows), :] = value[:, :128]
+    depth = rows * extra // 128
+    for i in range(128 // extra):
+        ref[pl.ds(rows, depth), i * extra:(i + 1) * extra] = value[i * depth:(i + 1) * depth, 128:]
+
+
+def unfold(ref, out):
+    rows, extra = out.shape[0], out.shape[1] - 128
+    out[:, :128] = ref[pl.ds(0, rows), :]
+    depth = rows * extra // 128
+    for i in range(128 // extra):
+        out[pl.ds(i * depth, depth), 128:] = ref[pl.ds(rows, depth), i * extra:(i + 1) * extra]
+
+
 SENDS = 96
 RECVS = 96
 HALO = 16
@@ -202,7 +218,7 @@
     trunk_ref, pout_ref,
     cw, wq, wk, wv, wo, pw,
     xin, xf, im, acc, accr, q1, q1r, hid, hall, s2, nrm, part, partr,
-    qo, ko, vo, qb, kb, vb, ao, at, ot, tin, eb, rowb, colb,
+    qo, ko, vo, qb, kb, vb, ao, at, vf, af, ot, tin, eb, rowb, colb,
     lsem, ssem, rsem,
 ):
     s, t, p = lax.axis_index("seq"), lax.axis_index("tp"), lax.axis_index("pr")
@@ -318,7 +334,7 @@
     square = jnp.zeros((rows, 1), f32)
     for c in range(chunks):
         cols = pl.ds(c * step, step)
-        rounded = gelu_tanh(accr[:, cols] * scale * cg_ref[:, cols]).astype(bf16)
+        rounded = gelu_tanh(accr[:, cols] * scale * cg_ref[cols][None, :]).astype(bf16)
         hid[:, cols] = rounded
         wide = rounded.astype(f32)
         square = square + jnp.sum(wide * wide, axis=1, keepdims=True)
@@ -335,6 +351,7 @@
     def _():
         hall[hmine, :] = hid[...]
 
+    gain = jnp.where(p == 0, ag_ref[pl.ds(0, half)][None, :], ag_ref[pl.ds(half, half)][None, :])
     for i in range(4):
         arrived(s2.at[i], r_s + i, me4 != i)
     for q in range(2):
@@ -342,7 +359,7 @@
             arrived(hall.at[pl.ds(q * rows, rows), pl.ds(c * step, step)], r_h + 2 * c + q, off | (p != q))
         scale = to_column(lax.rsqrt((s2[q] + s2[2 + q]) / width + EPSILON))
         block = pl.ds(q * rows, rows)
-        nrm[block, :] = (hall[block, :].astype(f32) * scale * ag_ref[p]).astype(bf16)
+        nrm[block, :] = (hall[block, :].astype(f32) * scale * gain).astype(bf16)
 
     for load in loads[1:]:
         load.wait()
@@ -352,7 +369,8 @@
     plan = [(wk, base_k, c) for c in range(qk // step)] + [
         (wv, base_v, c) for c in range(heads * HV // step)] + [(wq, base_q, c) for c in range(qk // step)]
     r_p = recvs.take(len(plan))
-    for i, (w, base, c) in enumerate(plan):
+    def multiply(i):
+        w, base, c = plan[i]
         cols = pl.ds(base + c * step, step)
         part[:, cols] = jnp.dot(nrm[...], w[:, c * step:(c + 1) * step], preferred_element_type=f32)
         remote(part.at[theirs, cols], partr.at[:, cols], r_p + i, partner)
@@ -374,19 +392,26 @@
 
     r_k, r_v, r_qq = recvs.take(n_seq), recvs.take(n_seq), recvs.take(n_seq)
     n_k, n_v = qk // step, heads * HV // step
-    for i in range(n_k):
+    last_k, last_v = n_k, n_k + n_v
+    for i in range(last_k + 1):
+        multiply(i)
+    for i in range(last_k):
         finish(i)
     for h in range(heads):
         ko[h] = total(base_k + h * QK, QK)
     scatter(ko, lambda j: kb.at[j, p], r_k)
     kb[s, p] = ko[s]
-    for i in range(n_k, n_k + n_v):
+    for i in range(last_k + 1, last_v + 1):
+        multiply(i)
+    for i in range(last_k, last_v):
         finish(i)
     for h in range(heads):
-        vo[h] = total(base_v + h * HV, HV)
+        fold(vo.at[h], total(base_v + h * HV, HV))
     scatter(vo, lambda j: vb.at[j, p], r_v)
     vb[s, p] = vo[s]
-    for i in range(n_k + n_v, len(plan)):
+    for i in range(last_v + 1, len(plan)):
+        multiply(i)
+    for i in range(last_v, len(plan)):
         finish(i)
     for h in range(heads):
         qo[h] = total(base_q + h * QK, QK)
@@ -409,21 +434,30 @@
     factor = 1.0 / math.sqrt(QK)
     r_a, r_a2 = recvs.take(n_seq), recvs.take(n_seq)
     keys_total = 2 * n_seq * rows
-    for d in far + (0,):
-        j = lax.rem(s + n_seq - d, n_seq)
-        if d:
-            arrived(qb.at[j], r_qq + d)
+    for j in range(n_seq):
+        for q in range(2):
+            unfold(vb.at[j, q], vf.at[j, q])
+    turns = far + (0,)
+    for first in range(0, n_seq, 2):
+        pair_of = turns[first:first + 2]
+        blocks = [lax.rem(s + n_seq - d, n_seq) for d in pair_of]
+        for d, j in zip(pair_of, blocks):
+            if d:
+                arrived(qb.at[j], r_qq + d)
         scores = lax.dot_general(
-            qb[j], kb[...].reshape(keys_total, QK), (((1,), (1,)), ((), ())), preferred_element_type=f32) * factor
+            jnp.concatenate([qb[j] for j in blocks], axis=0), kb[...].reshape(keys_total, QK),
+            (((1,), (1,)), ((), ())), preferred_element_type=f32) * factor
         weights = jnp.exp(scores - jnp.max(scores, axis=1, keepdims=True))
         sums = jnp.sum(weights, axis=1, keepdims=True)
-        mixed = jnp.dot(weights.astype(bf16), vb[...].reshape(keys_total, HV), preferred_element_type=f32)
+        mixed = jnp.dot(weights.astype(bf16), vf[...].reshape(keys_total, HV), preferred_element_type=f32)
         result = (mixed / sums).astype(bf16)
-        if d:
-            ao[d] = result
-            remote(ao.at[d], at.at[s, p], r_a + d, {"seq": j})
-        else:
-            at[s, p] = result
+        for i, (d, j) in enumerate(zip(pair_of, blocks)):
+            piece = result[i * rows:(i + 1) * rows]
+            if d:
+                fold(ao.at[d], piece)
+                remote(ao.at[d], at.at[s, p], r_a + d, {"seq": j})
+            else:
+                fold(at.at[s, p], piece)
     for d in (0,) + far[::-1]:
         h = lax.rem(s + d, n_seq)
         if d:
@@ -432,13 +466,16 @@
     for d in range(n_seq):
         arrived(at.at[lax.rem(s + d, n_seq), other_p], r_a2 + d)
 
+    for h in range(heads):
+        for q in range(2):
+            unfold(at.at[h, q], af.at[h, q])
     r_o = recvs.take(2 * chunks)
     for c in range(chunks):
         cols = pl.ds(c * step, step)
         value = jnp.zeros((2 * rows, step), f32)
         for h in range(heads):
             value = value + jnp.dot(
-                at[h].reshape(2 * rows, HV), wo[h * HV:(h + 1) * HV, cols], preferred_element_type=f32)
+                af[h].reshape(2 * rows, HV), wo[h * HV:(h + 1) * HV, cols], preferred_element_type=f32)
         ot[:, cols] = value.astype(bf16)
         remote(ot.at[theirs, cols], tin.at[t, :, cols], r_o + 2 * c + t, {"tp": p, "pr": other_p})
         remote(ot.at[own, cols], tin.at[t, :, cols], r_o + 2 * c + t, {"tp": p}, off)
@@ -514,11 +551,12 @@
     width = half * 2
     bf16, f32 = jnp.bfloat16, jnp.float32
     vmem = pl.BlockSpec(memory_space=pltpu.VMEM)
-    hbm = pl.BlockSpec(memory_space=pl.ANY)
+    hbm = pl.BlockSpec(memory_space=pltpu.HBM)
     flat_conv = conv_w.reshape(taps * cin, half)
     total = heads * (2 * QK + HV)
     pair = pair_in.shape[2]
     groups = rows // POOL
+    packed = rows * HV // 128
     v = pltpu.VMEM
     scratch = [
         v(flat_conv.shape, bf16), v(wq.shape, bf16), v(wk.shape, bf16), v(wv.shape, bf16), v(wo.shape, bf16),
@@ -527,9 +565,10 @@
         v((2 * rows, half), f32), v((rows, half), f32), v((8, rows), f32), v((8, rows), f32),
         v((rows, half), bf16), v((2 * rows, half), bf16), v((4, 8, rows), f32), v((2 * rows, half), bf16),
         v((2 * rows, total), f32), v((rows, total), f32),
-        v((heads, rows, QK), bf16), v((heads, rows, QK), bf16), v((heads, rows, HV), bf16),
-        v((heads, rows, QK), bf16), v((heads, 2, rows, QK), bf16), v((heads, 2, rows, HV), bf16),
-        v((heads, rows, HV), bf16), v((heads, 2, rows, HV), bf16),
+        v((heads, rows, QK), bf16), v((heads, rows, QK), bf16), v((heads, packed, 128), bf16),
+        v((heads, rows, QK), bf16), v((heads, 2, rows, QK), bf16), v((heads, 2, packed, 128), bf16),
+        v((heads, packed, 128), bf16), v((heads, 2, packed, 128), bf16),
+        v((heads, 2, rows, HV), bf16), v((heads, 2, rows, HV), bf16),
         v((2 * rows, half), bf16), v((2, rows, half), bf16),
         v((2, groups, pair), f32), v((2, groups, pair), f32), v((2, 4, groups, pair), f32),
         pltpu.SemaphoreType.DMA((8,)), pltpu.SemaphoreType.DMA((SENDS,)), pltpu.SemaphoreType.DMA((RECVS,)),
@@ -541,8 +580,8 @@
         out_specs=(vmem, vmem),
         scratch_shapes=scratch,
         compiler_params=pltpu.CompilerParams(
-            collective_id=0, has_side_effects=True, vmem_limit_bytes=60 * 1024 * 1024),
-    )(dna_feats, flat_conv, conv_gain.reshape(1, half), attn_gain.reshape(2, 1, half), wq, wk, wv, wo, pair_w,
+            collective_id=0, has_side_effects=True, vmem_limit_bytes=32 * 1024 * 1024),
+    )(dna_feats, flat_conv, conv_gain, attn_gain, wq, wk, wv, wo, pair_w,
       pair_in, pair_gain.reshape(1, pair), pair_w1, pair_w2)
 
 

time: 67.2 us -> 72.9 us (1.085)
  local copies, waits for them, and re-layouts: 5.66 us -> 14.4 us
  Pallas kernels: 60.6 us -> 57.3 us
    unnamed x2 -> x28, local copies, waits for them, and re-layouts: 3.09 us -> 14.4 us
    pallas_call x1, Pallas kernels: 60.6 us -> 57.3 us  [fused(): pl.pallas_call(fused_kernel, out_shape=(jax.ShapeDtypeStruct((rows, half)...]
    reshape x2 -> x0, local copies, waits for them, and re-layouts: 2.57 us -> none  [the longest x1 1.3 us: fused(): attn_gain.reshape(2, 1, half)]
where the time goes in v2:
time: 72.9 us; the launch traced here: 72.3 us
  Pallas kernels  57.3 us (79%)
  local copies, waits for them, and re-layouts  14.4 us (20%)
    pallas_call x1, Pallas kernels, fused(): pl.pallas_call(fused_kernel, out_shape=(jax.ShapeDtypeStruct((rows, half)...  57.3 us
    unnamed x28, local copies, waits for them, and re-layouts  14.4 us

profile of v2, /device:TPU:1, one launch (start us, length us, event | category | flops | bytes accessed | tf_op | source)
XLA Modules:
  0.0 72.3 jit_solution(10276624440722491311)
XLA Ops:
  0.6 0.0 copy-start
  0.6 1.8 %copy-done = bf16[5,384,768]{2,1,0:T(8,128)(2,1)S(1)} copy-done((bf16[5,384,768]{2,1,0:T(8,128)(2,1)S(1)}, bf16[5,384,768]{2,1,0:T(8,128)(2,1)}, u32[]{:S(2)}) %copy-start) | copy-done | bytes 2949144
  2.5 0.0 copy-start.1
  2.5 1.3 %copy-done.1 = bf16[768,768]{1,0:T(8,128)(2,1)S(1)} copy-done((bf16[768,768]{1,0:T(8,128)(2,1)S(1)}, bf16[768,768]{1,0:T(8,128)(2,1)}, u32[]{:S(2)}) %copy-start.1) | copy-done | bytes 1179672
  3.7 0.0 copy-start.2
  3.7 1.3 %copy-done.2 = bf16[768,768]{1,0:T(8,128)(2,1)S(1)} copy-done((bf16[768,768]{1,0:T(8,128)(2,1)S(1)}, bf16[768,768]{1,0:T(8,128)(2,1)}, u32[]{:S(2)}) %copy-start.2) | copy-done | bytes 1179672
  5.0 0.0 copy-start.3
  5.0 1.1 %copy-done.3 = bf16[768,512]{1,0:T(8,128)(2,1)S(1)} copy-done((bf16[768,512]{1,0:T(8,128)(2,1)S(1)}, bf16[768,512]{1,0:T(8,128)(2,1)}, u32[]{:S(2)}) %copy-start.3) | copy-done | bytes 786456
  6.1 0.0 copy-start.4
  6.1 1.1 %copy-done.4 = bf16[768,512]{1,0:T(8,128)(2,1)S(1)} copy-done((bf16[768,512]{1,0:T(8,128)(2,1)S(1)}, bf16[768,512]{1,0:T(8,128)(2,1)}, u32[]{:S(2)}) %copy-start.4) | copy-done | bytes 786456
  7.3 0.0 copy-start.5
  7.3 1.0 %copy-done.5 = bf16[768,256]{1,0:T(8,128)(2,1)S(1)} copy-done((bf16[768,256]{1,0:T(8,128)(2,1)S(1)}, bf16[768,256]{1,0:T(8,128)(2,1)}, u32[]{:S(2)}) %copy-start.5) | copy-done | bytes 393240
  8.3 0.0 copy-start.6
  8.3 0.9 %copy-done.6 = bf16[128,384]{1,0:T(8,128)(2,1)S(1)} copy-done((bf16[128,384]{1,0:T(8,128)(2,1)S(1)}, bf16[128,384]{1,0:T(8,128)(2,1)}, u32[]{:S(2)}) %copy-start.6) | copy-done | bytes 98328
  9.2 0.0 copy-start.7
  9.2 0.8 %copy-done.7 = bf16[8,32,128]{2,1,0:T(8,128)(2,1)S(1)} copy-done((bf16[8,32,128]{2,1,0:T(8,128)(2,1)S(1)}, bf16[8,32,128]{2,1,0:T(8,128)(2,1)}, u32[]{:S(2)}) %copy-start.7) | copy-done | bytes 65560
  10.0 0.0 copy-start.8
  10.0 0.8 %copy-done.8 = bf16[128,256]{1,0:T(8,128)(2,1)S(1)} copy-done((bf16[128,256]{1,0:T(8,128)(2,1)S(1)}, bf16[128,256]{1,0:T(8,128)(2,1)}, u32[]{:S(2)}) %copy-start.8) | copy-done | bytes 65560
  10.8 0.0 copy-start.9
  10.9 0.8 %copy-done.9 = bf16[256,128]{1,0:T(8,128)(2,1)S(1)} copy-done((bf16[256,128]{1,0:T(8,128)(2,1)S(1)}, bf16[256,128]{1,0:T(8,128)(2,1)}, u32[]{:S(2)}) %copy-start.9) | copy-done | bytes 65560
  11.7 0.0 copy-start.10
  11.7 0.7 copy-done.10
  12.4 0.0 copy-start.11
  12.4 0.7 copy-done.11
  13.1 0.0 copy-start.12
  13.1 0.7 copy-done.12
  13.7 57.3 %shard_map.140 = (bf16[128,768]{1,0:T(8,128)(2,1)S(1)}, bf16[8,32,128]{2,1,0:T(8,128)(2,1)S(1)}) custom-call(bf16[128,384]{1,0:T(8,128)(2,1)S(1)} %copy-done.6, bf16[1920,768]{1,0:T(8,128)(2,1)S(1)} %bitcast.2, f32[768]{0:T(1024)S(1)} %copy-done.11, f32[1536]{0:T(1024)S(1)} %copy-done.10, bf16[768,512]{1,0:T(8,128)(2,1)S(1)} %copy-done.3, ...), custom_call_target="tpu_custom_call" | custom-call | tf_op jit(solution)/shard_map/pallas_call | solution.py:576
  71.0 0.7 copy.17
  71.7 0.6 copy.18
Async XLA Ops:
  0.6 1.8 %copy-start = (bf16[5,384,768]{2,1,0:T(8,128)(2,1)S(1)}, bf16[5,384,768]{2,1,0:T(8,128)(2,1)}, u32[]{:S(2)}) copy-start(bf16[5,384,768]{2,1,0:T(8,128)(2,1)} %param.14) | copy-start | bytes 8847364
  2.5 1.3 %copy-start.1 = (bf16[768,768]{1,0:T(8,128)(2,1)S(1)}, bf16[768,768]{1,0:T(8,128)(2,1)}, u32[]{:S(2)}) copy-start(bf16[768,768]{1,0:T(8,128)(2,1)} %wv_hbm.1) | copy-start | bytes 3538948
  3.7 1.3 %copy-start.2 = (bf16[768,768]{1,0:T(8,128)(2,1)S(1)}, bf16[768,768]{1,0:T(8,128)(2,1)}, u32[]{:S(2)}) copy-start(bf16[768,768]{1,0:T(8,128)(2,1)} %wo_hbm.1) | copy-start | bytes 3538948
  5.0 1.1 %copy-start.3 = (bf16[768,512]{1,0:T(8,128)(2,1)S(1)}, bf16[768,512]{1,0:T(8,128)(2,1)}, u32[]{:S(2)}) copy-start(bf16[768,512]{1,0:T(8,128)(2,1)} %wq_hbm.1) | copy-start | bytes 2359300
  6.1 1.1 %copy-start.4 = (bf16[768,512]{1,0:T(8,128)(2,1)S(1)}, bf16[768,512]{1,0:T(8,128)(2,1)}, u32[]{:S(2)}) copy-start(bf16[768,512]{1,0:T(8,128)(2,1)} %wk_hbm.1) | copy-start | bytes 2359300
  7.3 1.0 %copy-start.5 = (bf16[768,256]{1,0:T(8,128)(2,1)S(1)}, bf16[768,256]{1,0:T(8,128)(2,1)}, u32[]{:S(2)}) copy-start(bf16[768,256]{1,0:T(8,128)(2,1)} %pw_hbm.1) | copy-start | bytes 1179652
  8.3 0.9 %copy-start.6 = (bf16[128,384]{1,0:T(8,128)(2,1)S(1)}, bf16[128,384]{1,0:T(8,128)(2,1)}, u32[]{:S(2)}) copy-start(bf16[128,384]{1,0:T(8,128)(2,1)} %x_ref.1) | copy-start | bytes 294916
  9.2 0.8 %copy-start.7 = (bf16[8,32,128]{2,1,0:T(8,128)(2,1)S(1)}, bf16[8,32,128]{2,1,0:T(8,128)(2,1)}, u32[]{:S(2)}) copy-start(bf16[8,32,128]{2,1,0:T(8,128)(2,1)} %pin_ref.1) | copy-start | bytes 196612
  10.0 0.8 %copy-start.8 = (bf16[128,256]{1,0:T(8,128)(2,1)S(1)}, bf16[128,256]{1,0:T(8,128)(2,1)}, u32[]{:S(2)}) copy-start(bf16[128,256]{1,0:T(8,128)(2,1)} %w1_ref.1) | copy-start | bytes 196612
  10.8 0.8 %copy-start.9 = (bf16[256,128]{1,0:T(8,128)(2,1)S(1)}, bf16[256,128]{1,0:T(8,128)(2,1)}, u32[]{:S(2)}) copy-start(bf16[256,128]{1,0:T(8,128)(2,1)} %w2_ref.1) | copy-start | bytes 196612
  11.7 0.7 copy-start.10
  12.4 0.7 copy-start.11
  13.1 0.7 copy-start.12

commit v3 on v2

--- a/solution.py
+++ b/solution.py
@@ -580,7 +580,7 @@
         out_specs=(vmem, vmem),
         scratch_shapes=scratch,
         compiler_params=pltpu.CompilerParams(
-            collective_id=0, has_side_effects=True, vmem_limit_bytes=32 * 1024 * 1024),
+            collective_id=0, has_side_effects=True, vmem_limit_bytes=60 * 1024 * 1024),
     )(dna_feats, flat_conv, conv_gain, attn_gain, wq, wk, wv, wo, pair_w,
       pair_in, pair_gain.reshape(1, pair), pair_w1, pair_w2)
 

time: 72.9 us -> 61.8 us (0.85)
  local copies, waits for them, and re-layouts: 14.4 us -> 3.09 us
    unnamed x28 -> x2, local copies, waits for them, and re-layouts: 14.4 us -> 3.09 us
where the time goes in v3:
time: 61.8 us; the launch traced here: 61.6 us
  Pallas kernels  57.9 us (94%)
  local copies, waits for them, and re-layouts  3.09 us (5%)
  between operations  0.64 us (1%)
    pallas_call x1, Pallas kernels, fused(): pl.pallas_call(fused_kernel, out_shape=(jax.ShapeDtypeStruct((rows, half)...  57.9 us
    unnamed x2, local copies, waits for them, and re-layouts  3.09 us

profile of v3, /device:TPU:1, one launch (start us, length us, event | category | flops | bytes accessed | tf_op | source)
XLA Modules:
  0.0 61.6 jit_solution(7979503822758950516)
XLA Ops:
  0.6 57.9 %shard_map.140 = (bf16[128,768]{1,0:T(8,128)(2,1)}, bf16[8,32,128]{2,1,0:T(8,128)(2,1)}) custom-call(bf16[128,384]{1,0:T(8,128)(2,1)} %x_ref.1, bf16[1920,768]{1,0:T(8,128)(2,1)} %bitcast.2, f32[768]{0:T(1024)} %cg_ref.1, f32[1536]{0:T(1024)} %ag_ref.1, bf16[768,512]{1,0:T(8,128)(2,1)} %wq_hbm.1, bf16[768,512]{1,0:T(8,128)(2,1)} %wk_hbm.1, ...), custom_call_target="tpu_custom_call" | custom-call | tf_op jit(solution)/shard_map/pallas_call | solution.py:576
  58.5 1.6 %copy.17 = bf16[128,768]{1,0:T(8,128)(2,1)} copy(bf16[128,768]{1,0:T(8,128)(2,1)} %get-tuple-element.4) | data formatting | bytes 393216
  60.2 1.5 %copy.18 = bf16[8,32,128]{2,1,0:T(8,128)(2,1)} copy(bf16[8,32,128]{2,1,0:T(8,128)(2,1)} %get-tuple-element.5) | data formatting | bytes 131072

commit v4 on v3

--- a/solution.py
+++ b/solution.py
@@ -218,7 +218,7 @@
     trunk_ref, pout_ref,
     cw, wq, wk, wv, wo, pw,
     xin, xf, im, acc, accr, q1, q1r, hid, hall, s2, nrm, part, partr,
-    qo, ko, vo, qb, kb, vb, ao, at, vf, af, ot, tin, eb, rowb, colb,
+    qo, ko, vo, qb, kb, vb, ao, at, vf, af, ws, ot, tin, eb, rowb, colb,
     lsem, ssem, rsem,
 ):
     s, t, p = lax.axis_index("seq"), lax.axis_index("tp"), lax.axis_index("pr")
@@ -367,7 +367,7 @@
     qk = heads * QK
     base_k, base_v, base_q = 0, qk, qk + heads * HV
     plan = [(wk, base_k, c) for c in range(qk // step)] + [
-        (wv, base_v, c) for c in range(heads * HV // step)] + [(wq, base_q, c) for c in range(qk // step)]
+        (wq, base_q, c) for c in range(qk // step)] + [(wv, base_v, c) for c in range(heads * HV // step)]
     r_p = recvs.take(len(plan))
     def multiply(i):
         w, base, c = plan[i]
@@ -391,8 +391,7 @@
             remote(src.at[h], dst_of(s), recv + d, {"seq": h})
 
     r_k, r_v, r_qq = recvs.take(n_seq), recvs.take(n_seq), recvs.take(n_seq)
-    n_k, n_v = qk // step, heads * HV // step
-    last_k, last_v = n_k, n_k + n_v
+    last_k, last_q = qk // step, 2 * qk // step
     for i in range(last_k + 1):
         multiply(i)
     for i in range(last_k):
@@ -401,43 +400,38 @@
         ko[h] = total(base_k + h * QK, QK)
     scatter(ko, lambda j: kb.at[j, p], r_k)
     kb[s, p] = ko[s]
-    for i in range(last_k + 1, last_v + 1):
+    for i in range(last_k + 1, last_q + 1):
         multiply(i)
-    for i in range(last_k, last_v):
+    for i in range(last_k, last_q):
+        finish(i)
+    for h in range(heads):
+        qo[h] = total(base_q + h * QK, QK)
+    scatter(qo, lambda j: qb.at[j], r_qq)
+    qb[s] = qo[s]
+    for i in range(last_q + 1, len(plan)):
+        multiply(i)
+    for i in range(last_q, len(plan)):
         finish(i)
     for h in range(heads):
         fold(vo.at[h], total(base_v + h * HV, HV))
     scatter(vo, lambda j: vb.at[j, p], r_v)
     vb[s, p] = vo[s]
-    for i in range(last_v + 1, len(plan)):
-        multiply(i)
-    for i in range(last_v, len(plan)):
-        finish(i)
-    for h in range(heads):
-        qo[h] = total(base_q + h * QK, QK)
-    scatter(qo, lambda j: qb.at[j], r_qq)
-    qb[s] = qo[s]
 
     r_k2, r_v2 = recvs.take(n_seq), recvs.take(n_seq)
     near = (0, 1, 3, 2) if n_seq == 4 else tuple(range(n_seq))
-    for buf, got, on in ((kb, r_k, r_k2), (vb, r_v, r_v2)):
-        for d in near:
-            j = lax.rem(s + n_seq - d, n_seq)
-            if d:
-                arrived(buf.at[j, p], got + d)
-            remote(buf.at[j, p], buf.at[j, p], on + d, partner)
-    for buf, on in ((kb, r_k2), (vb, r_v2)):
-        for d in near:
-            j = lax.rem(s + n_seq - d, n_seq)
-            arrived(buf.at[j, other_p], on + d)
+    for d in near:
+        j = lax.rem(s + n_seq - d, n_seq)
+        if d:
+            arrived(kb.at[j, p], r_k + d)
+        remote(kb.at[j, p], kb.at[j, p], r_k2 + d, partner)
+    for d in near:
+        arrived(kb.at[lax.rem(s + n_seq - d, n_seq), other_p], r_k2 + d)
 
     factor = 1.0 / math.sqrt(QK)
     r_a, r_a2 = recvs.take(n_seq), recvs.take(n_seq)
     keys_total = 2 * n_seq * rows
-    for j in range(n_seq):
-        for q in range(2):
-            unfold(vb.at[j, q], vf.at[j, q])
     turns = far + (0,)
+    scored = []
     for first in range(0, n_seq, 2):
         pair_of = turns[first:first + 2]
         blocks = [lax.rem(s + n_seq - d, n_seq) for d in pair_of]
@@ -448,8 +442,20 @@
             jnp.concatenate([qb[j] for j in blocks], axis=0), kb[...].reshape(keys_total, QK),
             (((1,), (1,)), ((), ())), preferred_element_type=f32) * factor
         weights = jnp.exp(scores - jnp.max(scores, axis=1, keepdims=True))
-        sums = jnp.sum(weights, axis=1, keepdims=True)
-        mixed = jnp.dot(weights.astype(bf16), vf[...].reshape(keys_total, HV), preferred_element_type=f32)
+        ws[first // 2] = weights.astype(bf16)
+        scored.append((pair_of, blocks, jnp.sum(weights, axis=1, keepdims=True)))
+    for d in near:
+        j = lax.rem(s + n_seq - d, n_seq)
+        if d:
+            arrived(vb.at[j, p], r_v + d)
+        remote(vb.at[j, p], vb.at[j, p], r_v2 + d, partner)
+        unfold(vb.at[j, p], vf.at[j, p])
+    for d in near:
+        j = lax.rem(s + n_seq - d, n_seq)
+        arrived(vb.at[j, other_p], r_v2 + d)
+        unfold(vb.at[j, other_p], vf.at[j, other_p])
+    for index, (pair_of, blocks, sums) in enumerate(scored):
+        mixed = jnp.dot(ws[index], vf[...].reshape(keys_total, HV), preferred_element_type=f32)
         result = (mixed / sums).astype(bf16)
         for i, (d, j) in enumerate(zip(pair_of, blocks)):
             piece = result[i * rows:(i + 1) * rows]
@@ -569,13 +575,14 @@
         v((heads, rows, QK), bf16), v((heads, 2, rows, QK), bf16), v((heads, 2, packed, 128), bf16),
         v((heads, packed, 128), bf16), v((heads, 2, packed, 128), bf16),
         v((heads, 2, rows, HV), bf16), v((heads, 2, rows, HV), bf16),
+        v((heads // 2, 2 * rows, 2 * heads * rows), bf16),
         v((2 * rows, half), bf16), v((2, rows, half), bf16),
         v((2, groups, pair), f32), v((2, groups, pair), f32), v((2, 4, groups, pair), f32),
         pltpu.SemaphoreType.DMA((8,)), pltpu.SemaphoreType.DMA((SENDS,)), pltpu.SemaphoreType.DMA((RECVS,)),
     ]
     return pl.pallas_call(
         fused_kernel,
-        out_shape=(jax.ShapeDtypeStruct((rows, half), bf16), jax.ShapeDtypeStruct(pair_in.shape, bf16)),
+        out_shape=(v((rows, half), bf16), v(pair_in.shape, bf16)),
         in_specs=[vmem, hbm, vmem, vmem, hbm, hbm, hbm, hbm, hbm, vmem, vmem, vmem, vmem],
         out_specs=(vmem, vmem),
         scratch_shapes=scratch,

time: 61.8 us -> 60.2 us (0.974)
  local copies, waits for them, and re-layouts: 3.09 us -> 1.31 us
    unnamed x2, local copies, waits for them, and re-layouts: 3.09 us -> 1.31 us
where the time goes in v4:
time: 60.2 us; the launch traced here: 60 us
  Pallas kernels  58.1 us (97%)
  local copies, waits for them, and re-layouts  1.31 us (2%)
  between operations  0.64 us (1%)
    pallas_call x1, Pallas kernels, fused(): pl.pallas_call(fused_kernel, out_shape=(v((rows, half), bf16), v(pair_in....  58.1 us
    unnamed x2, local copies, waits for them, and re-layouts  1.31 us

profile of v4, /device:TPU:1, one launch (start us, length us, event | category | flops | bytes accessed | tf_op | source)
XLA Modules:
  0.0 60.0 jit_solution(16095432093280326525)
XLA Ops:
  0.6 58.1 %shard_map.140 = (bf16[128,768]{1,0:T(8,128)(2,1)S(1)}, bf16[8,32,128]{2,1,0:T(8,128)(2,1)S(1)}) custom-call(bf16[128,384]{1,0:T(8,128)(2,1)} %x_ref.1, bf16[1920,768]{1,0:T(8,128)(2,1)} %bitcast.2, f32[768]{0:T(1024)} %cg_ref.1, f32[1536]{0:T(1024)} %ag_ref.1, bf16[768,512]{1,0:T(8,128)(2,1)} %wq_hbm.1, bf16[768,512]{1,0:T(8,128)(2,1)} %wk_hbm.1, ...), custom_call_target="tpu_custom_call" | custom-call | tf_op jit(solution)/shard_map/pallas_call | solution.py:583
  58.7 0.7 %copy.17 = bf16[128,768]{1,0:T(8,128)(2,1)} copy(bf16[128,768]{1,0:T(8,128)(2,1)S(1)} %get-tuple-element.2) | data formatting | bytes 393216
  59.4 0.6 %copy.18 = bf16[8,32,128]{2,1,0:T(8,128)(2,1)} copy(bf16[8,32,128]{2,1,0:T(8,128)(2,1)S(1)} %get-tuple-element.3) | data formatting | bytes 131072
